TPU v7x, 32 devices: a whole 2x2x4 slice. The times are simulated.
32 devices in a mesh: tp: 4 (over y, core), dp: 8 (over z, x).
Axes of the slice: x: 2, y: 2, z: 4, core: 2. Of those that a mesh axis runs over, the one named last changes fastest.
Arguments:
- tokens: bfloat16 [24, 1024, 768], P('dp', 'tp'), may hold values from -6 to 6
- lengths: int32 [24], P('dp'), may hold values from 196 to 1024, as said below
- ln_gain: float32 [768], replicated, may hold values from 0.1 to 1.9
- w_qkv: bfloat16 [768, 2304], P(None, 'tp'), may hold values from -0.21875 to 0.21875
- q_gain: float32 [12, 64], P('tp'), may hold values from 0.1 to 1.9
- k_gain: float32 [12, 64], P('tp'), may hold values from 0.1 to 1.9
- w_proj: bfloat16 [768, 768], P('tp'), may hold values from -1.75 to 1.75
- w_fc1: bfloat16 [768, 3072], P(None, 'tp'), may hold values from -0.21875 to 0.21875
- b_fc1: float32 [3072], P('tp'), may hold values from -3 to 3
- w_fc2: bfloat16 [3072, 768], P('tp'), may hold values from -0.109375 to 0.109375
- b_fc2: float32 [768], replicated, may hold values from -2 to 2
- d_out: bfloat16 [24, 1024, 768], P('dp', 'tp'), may hold values from -6 to 6
Outputs:
- output: bfloat16 [24, 1024, 768], P('dp', 'tp')
- d_tokens: float32 [24, 1024, 768], P('dp', 'tp')
- d_ln_gain: float32 [768], replicated
- d_qkv: float32 [768, 2304], P(None, 'tp')
- d_q_gain: float32 [12, 64], P('tp')
- d_k_gain: float32 [12, 64], P('tp')
- d_proj: float32 [768, 768], P('tp')
- d_fc1: float32 [768, 3072], P(None, 'tp')
- d_bias_one: float32 [3072], P('tp')
- d_fc2: float32 [3072, 768], P('tp')
- d_bias_two: float32 [768], replicated
Inputs may be any that keep to these rules, and one draw needn't show every extreme that they name: `lengths`: each image's length is one of 196, 576 and 1024; every draw holds all three.
All inputs are finite; a program needn't handle non-finite values.
Results may differ from a plain program's by a relative error of at most 0.014.
Values may be sent and summed in bfloat16 or wider, within the bound.
No kernel may reach another device: no remote copies, remote signals or barrier semaphores. Data moves between devices by JAX's collectives and lax.ppermute only.
A program may use at most 192 MiB of HBM per device.

v0:
```python
import jax
import jax.numpy as jnp
from jax import lax
from jax.sharding import PartitionSpec as P

epsilon = 1e-06
masked_value = -1e30


def layer_norm(values, scale_gain):
    average = jnp.mean(values, axis=-1, keepdims=True)
    centred = values - average
    variance = jnp.mean(centred * centred, axis=-1, keepdims=True)
    return centred * lax.rsqrt(variance + epsilon) * scale_gain


def gelu_exact(values):
    return jax.nn.gelu(values, approximate=False)


def score_block(queries, keys_normed, length, factor):
    scores = (
        jnp.einsum("qhd,khd->hqk", queries, keys_normed, preferred_element_type=jnp.float32)
        * factor
    )
    visible = lax.broadcasted_iota(jnp.int32, scores.shape, 2) < length
    return (scores, visible)


def forward_keys(factor, operands):
    queries, keys_normed, value_rows, length = operands
    scores, visible = score_block(queries, keys_normed, length, factor)
    masked = jnp.where(visible, scores, masked_value)
    row_peak = jnp.max(masked, axis=-1, keepdims=True)
    exponent = jnp.exp(masked - row_peak)
    row_total = jnp.sum(exponent, axis=-1, keepdims=True)
    probability = (exponent / row_total).astype(jnp.bfloat16)
    attended = jnp.einsum(
        "hqk,khd->qhd", probability, value_rows, preferred_element_type=jnp.float32
    )
    return (attended, row_peak[..., 0] + jnp.log(row_total[..., 0]))


def backward_keys(factor, operands):
    queries, keys_normed, value_rows, d_attended, logsum, length = operands
    scores, visible = score_block(queries, keys_normed, length, factor)
    probability = jnp.where(visible, jnp.exp(scores - logsum[..., None]), 0.0)
    d_probs = jnp.einsum("qhd,khd->hqk", d_attended, value_rows, preferred_element_type=jnp.float32)
    row_dot = jnp.sum(probability * d_probs, axis=-1, keepdims=True)
    d_scores = (probability * (d_probs - row_dot)).astype(jnp.bfloat16)
    d_queries = (
        jnp.einsum("hqk,khd->qhd", d_scores, keys_normed, preferred_element_type=jnp.float32)
        * factor
    )
    d_keys = (
        jnp.einsum("hqk,qhd->khd", d_scores, queries, preferred_element_type=jnp.float32) * factor
    )
    d_values = jnp.einsum(
        "hqk,qhd->khd",
        probability.astype(jnp.bfloat16),
        d_attended,
        preferred_element_type=jnp.float32,
    )
    return (d_queries, d_keys, d_values)


def shards(
    tokens, lengths, ln_gain, w_qkv, q_gain, k_gain, w_proj, w_fc1, b_fc1, w_fc2, b_fc2, d_out
):
    images = tokens.shape[0]
    heads_here = q_gain.shape[0]
    head_size = q_gain.shape[1]
    factor = head_size ** (-0.5)
    tokens_float = tokens.astype(jnp.float32)
    normed_local = layer_norm(tokens_float, ln_gain).astype(jnp.bfloat16)
    normed = lax.all_gather(normed_local, "tp", axis=1, tiled=True)
    seq_len = normed.shape[1]
    joined = jnp.einsum("bsd,dc->bsc", normed, w_qkv, preferred_element_type=jnp.float32)
    split_heads = joined.reshape(images, seq_len, heads_here, 3, head_size)
    query_raw = split_heads[:, :, :, 0]
    key_raw = split_heads[:, :, :, 1]
    queries = layer_norm(query_raw, q_gain).astype(jnp.bfloat16)
    keys_normed = layer_norm(key_raw, k_gain).astype(jnp.bfloat16)
    value_rows = split_heads[:, :, :, 2].astype(jnp.bfloat16)

    def attend_image(operands):
        return forward_keys(factor, operands)

    attended, logsum = lax.map(attend_image, (queries, keys_normed, value_rows, lengths))
    attended = attended.reshape(images, seq_len, heads_here * head_size).astype(jnp.bfloat16)
    hidden = jnp.einsum("bsd,df->bsf", normed, w_fc1, preferred_element_type=jnp.float32) + b_fc1
    active = gelu_exact(hidden).astype(jnp.bfloat16)
    partial_sum = jnp.einsum("bsc,cd->bsd", attended, w_proj, preferred_element_type=jnp.float32)
    partial_sum = partial_sum + jnp.einsum(
        "bsf,fd->bsd", active, w_fc2, preferred_element_type=jnp.float32
    )
    summed = lax.psum_scatter(
        partial_sum.astype(jnp.bfloat16), "tp", scatter_dimension=1, tiled=True
    ).astype(jnp.float32)
    output = (tokens_float + summed + b_fc2).astype(jnp.bfloat16)
    d_rows = lax.all_gather(d_out, "tp", axis=1, tiled=True)
    d_fc2 = jnp.einsum("bsf,bsd->fd", active, d_rows, preferred_element_type=jnp.float32)
    d_proj = jnp.einsum("bsc,bsd->cd", attended, d_rows, preferred_element_type=jnp.float32)
    d_active = jnp.einsum("bsd,fd->bsf", d_rows, w_fc2, preferred_element_type=jnp.float32)
    _, gelu_back = jax.vjp(gelu_exact, hidden)
    d_hidden = gelu_back(d_active)[0].astype(jnp.bfloat16)
    d_fc1 = jnp.einsum("bsd,bsf->df", normed, d_hidden, preferred_element_type=jnp.float32)
    d_bias_one = jnp.sum(d_hidden, axis=(0, 1), dtype=jnp.float32)
    d_normed = jnp.einsum("bsf,df->bsd", d_hidden, w_fc1, preferred_element_type=jnp.float32)
    d_attended = jnp.einsum(
        "bsd,cd->bsc", d_rows, w_proj, preferred_element_type=jnp.float32
    ).astype(jnp.bfloat16)
    d_heads = d_attended.reshape(images, seq_len, heads_here, head_size)

    def back_image(operands):
        return backward_keys(factor, operands)

    d_queries, d_keys, d_values = lax.map(
        back_image, (queries, keys_normed, value_rows, d_heads, logsum, lengths)
    )
    _, query_back = jax.vjp(layer_norm, query_raw, q_gain)
    d_query_raw, d_q_gain = query_back(d_queries)
    _, key_back = jax.vjp(layer_norm, key_raw, k_gain)
    d_key_raw, d_k_gain = key_back(d_keys)
    d_joined = (
        jnp.stack([d_query_raw, d_key_raw, d_values], axis=3)
        .reshape(images, seq_len, -1)
        .astype(jnp.bfloat16)
    )
    d_qkv = jnp.einsum("bsd,bsc->dc", normed, d_joined, preferred_element_type=jnp.float32)
    d_normed = d_normed + jnp.einsum(
        "bsc,dc->bsd", d_joined, w_qkv, preferred_element_type=jnp.float32
    )
    d_local = lax.psum_scatter(
        d_normed.astype(jnp.bfloat16), "tp", scatter_dimension=1, tiled=True
    ).astype(jnp.float32)
    _, norm_back = jax.vjp(layer_norm, tokens_float, ln_gain)
    d_tokens_part, d_ln_gain = norm_back(d_local)
    d_tokens = d_out.astype(jnp.float32) + d_tokens_part
    d_bias_two = jnp.sum(d_out, axis=(0, 1), dtype=jnp.float32)
    d_ln_gain, d_bias_two = lax.psum((d_ln_gain, d_bias_two), ("tp", "dp"))
    d_qkv, d_q_gain, d_k_gain, d_proj, d_fc1, d_bias_one, d_fc2 = (
        lax.psum(d_qkv.astype(jnp.bfloat16), "dp").astype(jnp.float32),
        lax.psum(d_q_gain.astype(jnp.bfloat16), "dp").astype(jnp.float32),
        lax.psum(d_k_gain.astype(jnp.bfloat16), "dp").astype(jnp.float32),
        lax.psum(d_proj.astype(jnp.bfloat16), "dp").astype(jnp.float32),
        lax.psum(d_fc1.astype(jnp.bfloat16), "dp").astype(jnp.float32),
        lax.psum(d_bias_one.astype(jnp.bfloat16), "dp").astype(jnp.float32),
        lax.psum(d_fc2.astype(jnp.bfloat16), "dp").astype(jnp.float32),
    )
    return (
        output,
        d_tokens,
        d_ln_gain,
        d_qkv,
        d_q_gain,
        d_k_gain,
        d_proj,
        d_fc1,
        d_bias_one,
        d_fc2,
        d_bias_two,
    )


def solution(mesh):
    placed = (
        P("dp", "tp", None),
        P("dp"),
        P(),
        P(None, "tp"),
        P("tp", None),
        P("tp", None),
        P("tp", None),
        P(None, "tp"),
        P("tp"),
        P("tp", None),
        P(),
        P("dp", "tp", None),
    )
    return jax.shard_map(
        shards,
        mesh=mesh,
        in_specs=placed,
        out_specs=(
            P("dp", "tp", None),
            P("dp", "tp", None),
            P(),
            P(None, "tp"),
            P("tp", None),
            P("tp", None),
            P("tp", None),
            P(None, "tp"),
            P("tp"),
            P("tp", None),
            P(),
        ),
        check_vma=False,
    )
```

profile of v0, /device:TPU:0, one launch (start us, length us, event | category | flops | bytes accessed | tf_op | source)
XLA Modules:
  0.0 569.2 jit_solution(9019446906122960374)
XLA Ops:
  17.7 36.0 %all-gather.3.cloned.1.call-done = bf16[3,1024,768]{2,1,0:T(8,128)(2,1)} async-done(((bf16[3,256,768]{2,1,0:T(8,128)(2,1)}), bf16[3,1024,768]{2,1,0:T(8,128)(2,1)}) %all-gather.3.cloned.1.call-update) | async-done | bytes 4718608 | tf_op jit(solution)/shard_map/all_gather | solution.py:76
  64.5 37.1 %while.28 = (s32[]{:T(128)}, bf16[3,1024,3,64]{1,3,2,0:T(8,128)(2,1)}, f32[3,3,1024]{2,1,0:T(4,128)}, bf16[3,1024,3,64]{1,3,2,0:T(8,128)(2,1)}, s32[3]{0:T(128)S...) while((s32[]{:T(128)}, bf16[3,1024,3,64]{1,3,2,0:T(8,128)(2,1)}, ...), condition=%wide.region_9.10_spmd.clone, body=%wide.region_6.9_spmd.sunk.clone | while | flops 843053056 | bytes 39823964 | solution.py:89
  101.6 6.0 %convolution_convert_fusion = bf16[3,1024,192]{1,2,0:T(8,128)(2,1)} fusion(bf16[3,1024,768]{2,1,0:T(8,128)(2,1)} %all-gather.5.cloned.1.call-done, bf16[192,768]{1,0:T(8,128)(2,1)} %param.22), kind=kOutput, calls=%fused_computation.126 | convolution fusion | flops 906559488 | bytes 6193152 | tf_op jit(solution)/shard_map/bsd,cd->bsc/dot_general | solution.py:110
  107.6 87.6 %while.29 = (s32[]{:T(128)}, f32[3,1024,3,64]{1,3,2,0:T(8,128)}, f32[3,1024,3,64]{1,3,2,0:T(8,128)}, bf16[3,1024,3,64]{1,3,2,0:T(8,128)(2,1)}, bf16[3,1024,3,64]...) while((s32[]{:T(128)}, f32[3,1024,3,64]{1,3,2,0:T(8,128)}, ...), condition=%wide.region_13.14_spmd.clone, body=%wide.region_11.13_spmd.sunk.clone | while | flops 2060843008 | bytes 124744848 | solution.py:118
  117.7 5.6 multiply_convert_fusion.6
  123.3 6.0 %fusion.164 = f32[3,1024,3,64]{1,3,2,0:T(8,128)} fusion(f32[3,1024,3,64]{1,3,2,0:T(8,128)} %get-tuple-element.364, s32[]{:T(128)} %get-tuple-element.362, bf16[3,1024,1024]{1,2,0:T(8,128)(2,1)} %multiply_convert_fusion.6, bf16[3,1024,3,64]{1,3,2,0:T(8,128)(2,1)} %get-tuple-element.378), kind=kOutput, calls=%fused_computation.31.clone.1.clone | convolution fusion | flops 402849792 | bytes 7472128 | tf_op jit(solution)/shard_map/while/body/eval_jaxpr/hqk,qhd->khd/dot_general | solution.py:56
  146.8 5.6 multiply_convert_fusion.6
  152.4 6.0 %fusion.164 = f32[3,1024,3,64]{1,3,2,0:T(8,128)} fusion(f32[3,1024,3,64]{1,3,2,0:T(8,128)} %get-tuple-element.364, s32[]{:T(128)} %get-tuple-element.362, bf16[3,1024,1024]{1,2,0:T(8,128)(2,1)} %multiply_convert_fusion.6, bf16[3,1024,3,64]{1,3,2,0:T(8,128)(2,1)} %get-tuple-element.378), kind=kOutput, calls=%fused_computation.31.clone.1.clone | convolution fusion | flops 402849792 | bytes 7472128 | tf_op jit(solution)/shard_map/while/body/eval_jaxpr/hqk,qhd->khd/dot_general | solution.py:56
  175.8 5.6 multiply_convert_fusion.6
  181.5 6.0 %fusion.164 = f32[3,1024,3,64]{1,3,2,0:T(8,128)} fusion(f32[3,1024,3,64]{1,3,2,0:T(8,128)} %get-tuple-element.364, s32[]{:T(128)} %get-tuple-element.362, bf16[3,1024,1024]{1,2,0:T(8,128)(2,1)} %multiply_convert_fusion.6, bf16[3,1024,3,64]{1,3,2,0:T(8,128)(2,1)} %get-tuple-element.378), kind=kOutput, calls=%fused_computation.31.clone.1.clone | convolution fusion | flops 402849792 | bytes 7472128 | tf_op jit(solution)/shard_map/while/body/eval_jaxpr/hqk,qhd->khd/dot_general | solution.py:56
  207.1 6.4 %fusion.72 = (u8[1024,768]{1,0:T(8,128)(4,1)S(1)}, u8[1024,768]{1,0:T(8,128)(4,1)S(1)}, f32[3,1024,768]{2,1,0:T(8,128)S(1)}) fusion(f32[768]{0:T(1024)S(1)} %copy-done.43, bf16[3,1024,768]{2,1,0:T(8,128)(2,1)S(1)} %bitcast.228, bf16[768,768]{1,0:T(8,128)(2,1)S(1)} %copy-done), kind=kOutput, calls=%fused_computation.122 | convolution fusion | flops 3655335936 | bytes 16911360 | tf_op jit(solution)/shard_map/bsd,df->bsf/dot_general | solution.py:91
  213.5 23.0 %multiply_convert_fusion.1 = (bf16[3,1024,768]{2,1,0:T(8,128)(2,1)S(1)}, f32[3,1024,768]{2,1,0:T(8,128)}) fusion(f32[3,1024,768]{2,1,0:T(8,128)S(1)} %get-tuple-element.172, f32[768]{0:T(1024)S(1)} %copy-done.43, u8[1024,768]{1,0:T(8,128)(4,1)S(1)} %get-tuple-element.109, u8[1024,768]{1,0:T(8,128)(4,1)S(1)} %get-tuple-element.108), kind=kLoop, calls=%fused_computation.70 | loop fusion | flops 167510016 | bytes 25168896 | tf_op jit(solution)/shard_map/convert_element_type | solution.py:92
  236.5 7.9 %bitcast_convert_fusion.2 = bf16[768,576]{0,1:T(8,128)(2,1)} fusion(bf16[3,1024,576]{1,2,0:T(8,128)(2,1)S(1)} %bitcast.224, bf16[3,1024,768]{2,1,0:T(8,128)(2,1)} %all-gather.3.cloned.1.call-done), kind=kOutput, calls=%fused_computation.125 | convolution fusion | flops 2718351360 | bytes 9142272 | tf_op jit(solution)/shard_map/bsd,bsc->dc/dot_general | solution.py:130
  249.0 14.2 %fusion.98 = (bf16[768]{0:T(1024)(128)(2,1)S(1)}, bf16[3,1024,768]{2,1,0:T(8,128)(2,1)}) fusion(f32[3,1024,768]{2,1,0:T(8,128)} %get-tuple-element.160, bf16[3,1024,768]{2,1,0:T(8,128)(2,1)} %all-gather.5.cloned.1.call-done, bf16[768,768]{1,0:T(8,128)(2,1)S(1)} %copy-done.44, f32[3,1024,768]{2,1,0:T(8,128)S(1)} %get-tuple-element.172, f32[768]{0:T(1024)S(1)} %copy-done.43), kind=kOutput, calls=%fused_computation.165 | convolution fusion | flops 3661626624 | bytes 29495808 | tf_op jit(solution)/shard_map/bsd,fd->bsf/dot_general | solution.py:104
  263.2 8.7 %bitcast_convert_fusion.1 = bf16[768,768]{1,0:T(8,128)(2,1)} fusion(bf16[3,1024,768]{2,1,0:T(8,128)(2,1)} %all-gather.3.cloned.1.call-done, bf16[3,1024,768]{2,1,0:T(8,128)(2,1)} %get-tuple-element.174), kind=kOutput, calls=%fused_computation.108 | convolution fusion | flops 3624468480 | bytes 10616832 | tf_op jit(solution)/shard_map/bsd,bsf->df/dot_general | solution.py:107
  271.9 7.3 %bitcast_convert_fusion = bf16[768,768]{1,0:T(8,128)(2,1)} fusion(bf16[3,1024,768]{2,1,0:T(8,128)(2,1)S(1)} %get-tuple-element.159, bf16[3,1024,768]{2,1,0:T(8,128)(2,1)} %all-gather.5.cloned.1.call-done), kind=kOutput, calls=%fused_computation.107 | convolution fusion | flops 3624468480 | bytes 10616832 | tf_op jit(solution)/shard_map/bsf,bsd->fd/dot_general | solution.py:102
  279.3 5.9 %fusion.81 = f32[3,1024,768]{2,1,0:T(8,128)S(1)} fusion(bf16[3,1024,768]{2,1,0:T(8,128)(2,1)} %get-tuple-element.174, bf16[768,768]{1,0:T(8,128)(2,1)S(1)} %copy-done), kind=kOutput, calls=%fused_computation.136 | convolution fusion | flops 3623878656 | bytes 15335424 | tf_op jit(solution)/shard_map/bsf,df->bsd/dot_general | solution.py:109
  285.3 5.6 add_convert_fusion
  291.0 6.1 %fusion.79 = f32[3,1024,768]{2,1,0:T(8,128)S(1)} fusion(bf16[3,1024,768]{2,1,0:T(8,128)(2,1)} %copy-done.13, bf16[768,768]{1,0:T(8,128)(2,1)S(1)} %copy-done.44), kind=kOutput, calls=%fused_computation.134 | convolution fusion | flops 3623878656 | bytes 15335424 | tf_op jit(solution)/shard_map/bsf,fd->bsd/dot_general | solution.py:94
  302.0 22.5 %all-reduce.1 = (bf16[3,64]{1,0:T(4,128)(2,1)S(1)}, bf16[3,64]{1,0:T(4,128)(2,1)S(1)}, bf16[768]{0:T(1024)(128)(2,1)S(1)}) all-reduce(bf16[3,64]{1,0:T(4,128)(2,1)S(1)} %get-tuple-element.176, bf16[3,64]{1,0:T(4,128)(2,1)S(1)} %get-tuple-element.110, bf16[768]{0:T(1024)(128)(2,1)S(1)} %get-tuple-element.173), channel_id=1, replica_groups=mesh['tp'=4,'dp'=8] {'dp'}, use_global_device_ids=true, to_apply=%region_25.26 | all-reduce | flops 1152 | bytes 4608 | tf_op jit(solution)/shard_map/psum | solution.py:144
  326.3 92.2 %all-reduce.5.cloned.1.call-done = (bf16[768,576]{0,1:T(8,128)(2,1)}, bf16[192,768]{1,0:T(8,128)(2,1)}, bf16[768,768]{1,0:T(8,128)(2,1)}, bf16[768,768]{1,0:T(8,128)(2,1)}) async-done(((bf16[768,576]{0,1:T(8,128)(2,1)}, bf16[192,768]{1,0:T(8,128)(2,1)}, bf16[768,768]{1,0:T(8,128)(2,1)}, bf16[768,768]{1,0:T(8,128)(2,1)}), (bf16[768,576]{0,1:T(8,128)(2,1)}, bf16[192,768]{1,0:T(8,128)(2,1)}, ...) | async-done | bytes 3538960 | tf_op jit(solution)/shard_map/psum | solution.py:143
  425.3 42.6 %reduce-scatter.5.cloned.1.call-done = bf16[3,256,768]{2,1,0:T(8,128)(2,1)} async-done(((bf16[3,1024,768]{2,1,0:T(8,128)(2,1)}), bf16[3,256,768]{2,1,0:T(8,128)(2,1)}) %reduce-scatter.5.cloned.1.call-update) | async-done | bytes 1179664 | tf_op jit(solution)/shard_map/reduce_scatter | solution.py:134
  473.1 45.0 %reduce-scatter.3.cloned.1.call-done = bf16[3,256,768]{2,1,0:T(8,128)(2,1)} async-done(((bf16[3,1024,768]{2,1,0:T(8,128)(2,1)}), bf16[3,256,768]{2,1,0:T(8,128)(2,1)}) %reduce-scatter.3.cloned.1.call-update) | async-done | bytes 1179664 | tf_op jit(solution)/shard_map/reduce_scatter | solution.py:97
  522.6 39.6 %all-reduce = (f32[768]{0:T(1024)}, f32[768]{0:T(1024)}) all-reduce(f32[768]{0:T(1024)} %get-tuple-element.114, f32[768]{0:T(1024)} %get-tuple-element.169), channel_id=1, replica_groups=mesh['tp'=4,'dp'=8] {'tp','dp'}, use_global_device_ids=true, to_apply=%region_22.23 | all-reduce | flops 1536 | bytes 12288 | tf_op jit(solution)/shard_map/psum | solution.py:141
  (203 shorter events, 150.2 us)
Async XLA Ops:
  7.2 199.6 %copy-start = (bf16[768,768]{1,0:T(8,128)(2,1)S(1)}, bf16[768,768]{1,0:T(8,128)(2,1)}, u32[]{:S(2)}) copy-start(bf16[768,768]{1,0:T(8,128)(2,1)} %param.23) | copy-start | bytes 3538948
  7.2 4.7 copy-start.6
  7.2 46.4 %all-gather.3.cloned.1.call-start = ((), (), s32[]{:S(2)}) async-start(), calls=%async_computation.2 | async-start | bytes 5898240 | tf_op jit(solution)/shard_map/all_gather | solution.py:76
  13.3 40.3 %copy-start.45 = (bf16[768,576]{0,1:T(8,128)(2,1)S(1)}, bf16[768,576]{0,1:T(8,128)(2,1)}, u32[]{:S(2)}) copy-start(bf16[768,576]{0,1:T(8,128)(2,1)} %param.19) | copy-start | bytes 2654212
  13.3 88.3 %all-gather.5.cloned.1.call-start = ((), (), s32[]{:S(2)}) async-start(), calls=%async_computation.4 | async-start | bytes 5898240 | tf_op jit(solution)/shard_map/all_gather | solution.py:101
  14.1 404.4 %all-reduce.5.cloned.1.call-start = ((), (), s32[]{:S(2)}) async-start(), calls=%async_computation.6 | async-start | bytes 7077888 | tf_op jit(solution)/shard_map/psum | solution.py:143
  101.6 6.0 %copy-start.8 = (bf16[3,1024,3,64]{1,3,2,0:T(8,128)(2,1)}, bf16[3,1024,3,64]{1,3,2,0:T(8,128)(2,1)S(1)}, u32[]{:S(2)}) copy-start(bf16[3,1024,3,64]{1,3,2,0:T(8,128)(2,1)S(1)} %get-tuple-element.394) | copy-start | bytes 3538948
  101.6 6.0 %copy-start.9 = (bf16[3,1024,3,64]{1,3,2,0:T(8,128)(2,1)}, bf16[3,1024,3,64]{1,3,2,0:T(8,128)(2,1)S(1)}, u32[]{:S(2)}) copy-start(bf16[3,1024,3,64]{1,3,2,0:T(8,128)(2,1)S(1)} %get-tuple-element.395) | copy-start | bytes 3538948
  107.6 87.6 %copy-start.5 = (f32[3,1024,3,1,64]{1,4,3,2,0:T(8,128)S(1)}, f32[3,1024,3,1,64]{1,4,3,2,0:T(8,128)}, u32[]{:S(2)}) copy-start(f32[3,1024,3,1,64]{1,4,3,2,0:T(8,128)} %copy-done.4) | copy-start | bytes 7077892
  107.6 87.6 %copy-start.40 = (f32[3,64]{1,0:T(4,128)S(1)}, f32[3,64]{1,0:T(4,128)}, u32[]{:S(2)}) copy-start(f32[3,64]{1,0:T(4,128)} %param.20) | copy-start | bytes 2308
  123.3 6.0 %copy-start.1 = (bf16[3,1024,1024]{1,2,0:T(8,128)(2,1)S(1)}, bf16[3,1024,1024]{1,2,0:T(8,128)(2,1)}, u32[]{:S(2)}) copy-start(bf16[3,1024,1024]{1,2,0:T(8,128)(2,1)} %multiply_convert_fusion.6) | copy-start | bytes 18874372 | tf_op jit(solution)/shard_map/while
  152.4 6.0 %copy-start.1 = (bf16[3,1024,1024]{1,2,0:T(8,128)(2,1)S(1)}, bf16[3,1024,1024]{1,2,0:T(8,128)(2,1)}, u32[]{:S(2)}) copy-start(bf16[3,1024,1024]{1,2,0:T(8,128)(2,1)} %multiply_convert_fusion.6) | copy-start | bytes 18874372 | tf_op jit(solution)/shard_map/while
  181.5 6.0 %copy-start.1 = (bf16[3,1024,1024]{1,2,0:T(8,128)(2,1)S(1)}, bf16[3,1024,1024]{1,2,0:T(8,128)(2,1)}, u32[]{:S(2)}) copy-start(bf16[3,1024,1024]{1,2,0:T(8,128)(2,1)} %multiply_convert_fusion.6) | copy-start | bytes 18874372 | tf_op jit(solution)/shard_map/while
  207.1 29.4 %copy-start.14 = (bf16[3,1024,3,3,64]{1,4,3,2,0:T(8,128)(2,1)}, bf16[3,1024,3,3,64]{1,4,3,2,0:T(8,128)(2,1)S(1)}, u32[]{:S(2)}) copy-start(bf16[3,1024,3,3,64]{1,4,3,2,0:T(8,128)(2,1)S(1)} %copy.30) | copy-start | bytes 10616836
  236.5 35.4 %copy-start.13 = (bf16[3,1024,768]{2,1,0:T(8,128)(2,1)}, bf16[3,1024,768]{2,1,0:T(8,128)(2,1)S(1)}, u32[]{:S(2)}) copy-start(bf16[3,1024,768]{2,1,0:T(8,128)(2,1)S(1)} %get-tuple-element.159) | copy-start | bytes 14155780
  279.2 6.0 %copy-start.46 = (bf16[768,576]{0,1:T(8,128)(2,1)S(1)}, bf16[768,576]{0,1:T(8,128)(2,1)}, u32[]{:S(2)}) copy-start(bf16[768,576]{0,1:T(8,128)(2,1)} %param.19) | copy-start | bytes 2654212
  279.3 188.6 %reduce-scatter.5.cloned.1.call-start = ((), (), s32[]{:S(2)}) async-start(), calls=%async_computation.5 | async-start | bytes 5898240 | tf_op jit(solution)/shard_map/reduce_scatter | solution.py:134
  279.3 6.0 %copy-start.15 = (bf16[3,1024,3,3,64]{1,4,3,2,0:T(8,128)(2,1)S(1)}, bf16[3,1024,3,3,64]{1,4,3,2,0:T(8,128)(2,1)}, u32[]{:S(2)}) copy-start(bf16[3,1024,3,3,64]{1,4,3,2,0:T(8,128)(2,1)} %copy-done.14) | copy-start | bytes 10616836
  290.9 6.1 %copy-start.31 = (bf16[192,768]{1,0:T(8,128)(2,1)S(1)}, bf16[192,768]{1,0:T(8,128)(2,1)}, u32[]{:S(2)}) copy-start(bf16[192,768]{1,0:T(8,128)(2,1)} %param.22) | copy-start | bytes 884740
  291.0 227.1 %reduce-scatter.3.cloned.1.call-start = ((), (), s32[]{:S(2)}) async-start(), calls=%async_computation.3 | async-start | bytes 5898240 | tf_op jit(solution)/shard_map/reduce_scatter | solution.py:97
  423.0 44.8 %copy-start.7 = (bf16[3,256,768]{2,1,0:T(8,128)(2,1)S(1)}, bf16[3,256,768]{2,1,0:T(8,128)(2,1)}, u32[]{:S(2)}) copy-start(bf16[3,256,768]{2,1,0:T(8,128)(2,1)} %param.16) | copy-start | bytes 3538948
  423.0 44.8 %copy-start.33 = (f32[3,256]{1,0:T(4,128)S(1)}, f32[3,256]{1,0:T(4,128)}, u32[]{:S(2)}) copy-start(f32[3,256]{1,0:T(4,128)} %copy-done.32) | copy-start | bytes 9220
  423.1 44.8 %copy-start.35 = (f32[768]{0:T(1024)S(1)}, f32[768]{0:T(1024)}, u32[]{:S(2)}) copy-start(f32[768]{0:T(1024)} %param.18) | copy-start | bytes 9220
  423.1 47.5 %copy-start.37 = (f32[3,256]{1,0:T(4,128)S(1)}, f32[3,256]{1,0:T(4,128)}, u32[]{:S(2)}) copy-start(f32[3,256]{1,0:T(4,128)} %copy-done.36) | copy-start | bytes 9220
  (33 other events, 70.5 us)
Sparse Core Ops, SparseCore 0:
  13.5 40.1 all-gather.2
  55.2 37.4 all-gather.4
  279.4 139.1 all-reduce.4
  420.9 46.8 reduce-scatter.4
  470.2 47.8 reduce-scatter.2
where the time goes:
time: 580 us; the launch traced here: 569 us
  waiting for transfers between devices  216 us (37%)
  matrix products  169 us (29%)
  other arithmetic  91.3 us (16%)
  blocking collectives  62.1 us (11%)
  local copies, waits for them, and re-layouts  15.1 us (3%)
  between operations  14.8 us (3%)
    psum x1, waiting for transfers between devices, shards(): lax.psum(d_qkv.astype(jnp.bfloat16), 'dp').astype(jnp.float32)  92.2 us
    reduce_scatter x1, waiting for transfers between devices, shards(): lax.psum_scatter(partial_sum.astype(jnp.bfloat16), 'tp', scatter_dimensio...  45 us
    reduce_scatter x1, waiting for transfers between devices, shards(): lax.psum_scatter(d_normed.astype(jnp.bfloat16), 'tp', scatter_dimension=1...  42.6 us
    psum x1, blocking collectives, shards(): d_ln_gain, d_bias_two = lax.psum((d_ln_gain, d_bias_two), ('tp', 'dp'))  39.6 us
    all_gather x1, waiting for transfers between devices, shards(): normed = lax.all_gather(normed_local, 'tp', axis=1, tiled=True)  36 us
    convert_element_type x1, other arithmetic, shards(): active = gelu_exact(hidden).astype(jnp.bfloat16)  23 us
    psum x1, blocking collectives, shards(): lax.psum(d_q_gain.astype(jnp.bfloat16), 'dp').astype(jnp.float32)  22.5 us
    dot_general x3, matrix products, backward_keys(): jnp.einsum('hqk,qhd->khd', d_scores, queries, preferred_element_type=jnp....  17.9 us
  transfers between devices with their start and end apart: 5, of which 4 were waited for; matrix products, arithmetic and copies ran while one was open for 15% of the time, Pallas kernels for 0%

commit v1 on v0

--- a/solution.py
+++ b/solution.py
@@ -1,3 +1,4 @@
+import functools
 import jax
 import jax.numpy as jnp
 from jax import lax
@@ -5,6 +6,37 @@
 
 epsilon = 1e-06
 masked_value = -1e30
+
+
+def _produce_units(my_data, row_axis, d0):
+    raw_out, w_next, arr_next = (
+        lax.axis_size(row_axis),
+        lax.axis_index(row_axis),
+        my_data.shape[d0],
+    )
+    column = [u * raw_out if at == d0 else u for at, u in enumerate(my_data.shape)]
+    finding = lax.dynamic_update_slice_in_dim(
+        jnp.zeros(column, my_data.dtype), my_data, w_next * arr_next, axis=d0
+    )
+    odd = d_next = my_data
+    for c in range(1, raw_out // 2 + 1):
+        odd = lax.ppermute(
+            odd, row_axis, list(map(lambda at: (at, (at + 1) % raw_out), range(raw_out)))
+        )
+        finding = lax.dynamic_update_slice_in_dim(
+            finding, odd, (w_next - c) % raw_out * arr_next, axis=d0
+        )
+        if 2 * c < raw_out:
+            d_next = lax.ppermute(
+                d_next, row_axis, list(map(lambda at: (at, (at - 1) % raw_out), range(raw_out)))
+            )
+            finding = lax.dynamic_update_slice_in_dim(
+                finding, d_next, (w_next + c) % raw_out * arr_next, axis=d0
+            )
+    return finding
+
+
+save_the_figure = functools.partial(_produce_units, row_axis="tp", d0=1)
 
 
 def layer_norm(values, scale_gain):
@@ -73,7 +105,7 @@
     factor = head_size ** (-0.5)
     tokens_float = tokens.astype(jnp.float32)
     normed_local = layer_norm(tokens_float, ln_gain).astype(jnp.bfloat16)
-    normed = lax.all_gather(normed_local, "tp", axis=1, tiled=True)
+    normed = save_the_figure(normed_local)
     seq_len = normed.shape[1]
     joined = jnp.einsum("bsd,dc->bsc", normed, w_qkv, preferred_element_type=jnp.float32)
     split_heads = joined.reshape(images, seq_len, heads_here, 3, head_size)

time: 580 us -> 598 us (1.031)
  local copies, waits for them, and re-layouts: 15.1 us -> 30.5 us
    all_gather x1 -> x0, waiting for transfers between devices: 36 us -> none  [shards(): normed = lax.all_gather(normed_local, 'tp', axis=1, tiled=True)]
    ppermute x0 -> x3, waiting for transfers between devices: none -> 25.7 us  [the longest x2 25.7 us: _produce_units(): lax.ppermute(odd, row_axis, list(map(lambda at: (at, (at + 1) % raw_out),...]
  transfers between devices with their start and end apart: 5 -> 7, of which waited for: 4 -> 5; matrix products, arithmetic and copies ran while one was open for 15% -> 22% of each run, Pallas kernels for 0% -> 0%
where the time goes in v1:
time: 598 us; the launch traced here: 591 us
  waiting for transfers between devices  211 us (35%)
  matrix products  171 us (29%)
  other arithmetic  89.8 us (15%)
  blocking collectives  67.8 us (11%)
  local copies, waits for them, and re-layouts  30.5 us (5%)
  between operations  15 us (3%)
    psum x1, waiting for transfers between devices, shards(): lax.psum(d_qkv.astype(jnp.bfloat16), 'dp').astype(jnp.float32)  98 us
    reduce_scatter x1, waiting for transfers between devices, shards(): lax.psum_scatter(partial_sum.astype(jnp.bfloat16), 'tp', scatter_dimensio...  45 us
    reduce_scatter x1, waiting for transfers between devices, shards(): lax.psum_scatter(d_normed.astype(jnp.bfloat16), 'tp', scatter_dimension=1...  42.7 us
    psum x1, blocking collectives, shards(): d_ln_gain, d_bias_two = lax.psum((d_ln_gain, d_bias_two), ('tp', 'dp'))  39.6 us
    psum x1, blocking collectives, shards(): lax.psum(d_q_gain.astype(jnp.bfloat16), 'dp').astype(jnp.float32)  28.2 us
    ppermute x2, waiting for transfers between devices, _produce_units(): lax.ppermute(odd, row_axis, list(map(lambda at: (at, (at + 1) % raw_out),...  25.7 us
    convert_element_type x1, other arithmetic, shards(): active = gelu_exact(hidden).astype(jnp.bfloat16)  23 us
    dot_general x3, matrix products, backward_keys(): jnp.einsum('hqk,qhd->khd', d_scores, queries, preferred_element_type=jnp....  17.9 us
  transfers between devices with their start and end apart: 7, of which 5 were waited for; matrix products, arithmetic and copies ran while one was open for 22% of the time, Pallas kernels for 0%

profile of v1, /device:TPU:0, one launch (start us, length us, event | category | flops | bytes accessed | tf_op | source)
XLA Modules:
  0.0 591.1 jit_solution(9031071793622279805)
XLA Ops:
  14.3 24.0 %collective-permute-done = bf16[3,256,768]{2,1,0:T(8,128)(2,1)} collective-permute-done((bf16[3,256,768]{2,1,0:T(8,128)(2,1)S(1)}, bf16[3,256,768]{2,1,0:T(8,128)(2,1)}, u32[]{:S(2)}, u32[]{:S(2)}) %collective-permute-start) | collective-permute-done | bytes 1179680 | tf_op jit(solution)/shard_map/ppermute | solution.py:23
  69.3 37.3 %while.28 = (s32[]{:T(128)}, bf16[3,1024,3,64]{1,3,2,0:T(8,128)(2,1)}, f32[3,3,1024]{2,1,0:T(4,128)}, bf16[3,1024,3,64]{1,3,2,0:T(8,128)(2,1)}, s32[3]{0:T(128)S...) while((s32[]{:T(128)}, bf16[3,1024,3,64]{1,3,2,0:T(8,128)(2,1)}, ...), condition=%wide.region_9.10_spmd.clone, body=%wide.region_6.9_spmd.sunk.clone | while | flops 843053056 | bytes 39823964 | solution.py:121
  106.6 9.3 %fusion.72 = (u8[1024,768]{1,0:T(8,128)(4,1)S(1)}, u8[1024,768]{1,0:T(8,128)(4,1)S(1)}, f32[3,1024,768]{2,1,0:T(8,128)S(1)}) fusion(f32[768]{0:T(1024)S(1)} %copy-done.44, bf16[3,1024,768]{1,2,0:T(8,128)(2,1)} %constant_dynamic-update-slice_fusion, bf16[768,768]{1,0:T(8,128)(2,1)S(1)} %copy-done), kind=kOutput, calls=%fused_computation.122 | convolution fusion | flops 3655335936 | bytes 16911360 | tf_op jit(solution)/shard_map/bsd,df->bsf/dot_general | solution.py:123
  119.6 23.0 %multiply_convert_fusion.1 = (bf16[3,1024,768]{2,1,0:T(8,128)(2,1)}, f32[3,1024,768]{2,1,0:T(8,128)}) fusion(f32[3,1024,768]{2,1,0:T(8,128)S(1)} %get-tuple-element.172, f32[768]{0:T(1024)S(1)} %copy-done.44, u8[1024,768]{1,0:T(8,128)(4,1)S(1)} %get-tuple-element.109, u8[1024,768]{1,0:T(8,128)(4,1)S(1)} %get-tuple-element.108), kind=kLoop, calls=%fused_computation.70 | loop fusion | flops 167510016 | bytes 25168896 | tf_op jit(solution)/shard_map/convert_element_type | solution.py:124
  142.6 5.0 convolution_convert_fusion
  147.6 88.0 %while.29 = (s32[]{:T(128)}, f32[3,1024,3,64]{1,3,2,0:T(8,128)}, f32[3,1024,3,64]{1,3,2,0:T(8,128)}, bf16[3,1024,3,64]{1,3,2,0:T(8,128)(2,1)}, bf16[3,1024,3,64]...) while((s32[]{:T(128)}, f32[3,1024,3,64]{1,3,2,0:T(8,128)}, ...), condition=%wide.region_13.14_spmd.clone, body=%wide.region_11.13_spmd.sunk.clone | while | flops 2060843008 | bytes 124744848 | solution.py:150
  157.9 5.7 multiply_convert_fusion.6
  163.6 6.0 %fusion.164 = f32[3,1024,3,64]{1,3,2,0:T(8,128)} fusion(f32[3,1024,3,64]{1,3,2,0:T(8,128)} %get-tuple-element.364, s32[]{:T(128)} %get-tuple-element.362, bf16[3,1024,1024]{1,2,0:T(8,128)(2,1)} %multiply_convert_fusion.6, bf16[3,1024,3,64]{1,3,2,0:T(8,128)(2,1)} %get-tuple-element.378), kind=kOutput, calls=%fused_computation.31.clone.1.clone | convolution fusion | flops 402849792 | bytes 7472128 | tf_op jit(solution)/shard_map/while/body/eval_jaxpr/hqk,qhd->khd/dot_general | solution.py:88
  187.1 5.7 multiply_convert_fusion.6
  192.8 6.0 %fusion.164 = f32[3,1024,3,64]{1,3,2,0:T(8,128)} fusion(f32[3,1024,3,64]{1,3,2,0:T(8,128)} %get-tuple-element.364, s32[]{:T(128)} %get-tuple-element.362, bf16[3,1024,1024]{1,2,0:T(8,128)(2,1)} %multiply_convert_fusion.6, bf16[3,1024,3,64]{1,3,2,0:T(8,128)(2,1)} %get-tuple-element.378), kind=kOutput, calls=%fused_computation.31.clone.1.clone | convolution fusion | flops 402849792 | bytes 7472128 | tf_op jit(solution)/shard_map/while/body/eval_jaxpr/hqk,qhd->khd/dot_general | solution.py:88
  216.2 5.7 multiply_convert_fusion.6
  221.9 6.0 %fusion.164 = f32[3,1024,3,64]{1,3,2,0:T(8,128)} fusion(f32[3,1024,3,64]{1,3,2,0:T(8,128)} %get-tuple-element.364, s32[]{:T(128)} %get-tuple-element.362, bf16[3,1024,1024]{1,2,0:T(8,128)(2,1)} %multiply_convert_fusion.6, bf16[3,1024,3,64]{1,3,2,0:T(8,128)(2,1)} %get-tuple-element.378), kind=kOutput, calls=%fused_computation.31.clone.1.clone | convolution fusion | flops 402849792 | bytes 7472128 | tf_op jit(solution)/shard_map/while/body/eval_jaxpr/hqk,qhd->khd/dot_general | solution.py:88
  246.8 7.8 %bitcast_convert_fusion.2 = bf16[768,576]{0,1:T(8,128)(2,1)} fusion(bf16[3,1024,768]{1,2,0:T(8,128)(2,1)} %constant_dynamic-update-slice_fusion, bf16[3,1024,576]{1,2,0:T(8,128)(2,1)S(1)} %bitcast.228), kind=kOutput, calls=%fused_computation.125 | convolution fusion | flops 2718351360 | bytes 9142272 | tf_op jit(solution)/shard_map/bsd,bsc->dc/dot_general | solution.py:162
  254.7 14.3 %fusion.98 = (bf16[768]{0:T(1024)(128)(2,1)S(1)}, bf16[3,1024,768]{2,1,0:T(8,128)(2,1)}) fusion(f32[3,1024,768]{2,1,0:T(8,128)} %get-tuple-element.160, bf16[3,1024,768]{2,1,0:T(8,128)(2,1)} %all-gather.2.cloned.1.call-done, bf16[768,768]{1,0:T(8,128)(2,1)S(1)} %copy-done.46, f32[3,1024,768]{2,1,0:T(8,128)S(1)} %bitcast.223, f32[768]{0:T(1024)S(1)} %copy-done.45), kind=kOutput, calls=%fused_computation.169 | convolution fusion | flops 3661626624 | bytes 29495808 | tf_op jit(solution)/shard_map/bsd,fd->bsf/dot_general | solution.py:136
  269.0 8.6 %bitcast_convert_fusion.1 = bf16[768,768]{1,0:T(8,128)(2,1)} fusion(bf16[3,1024,768]{1,2,0:T(8,128)(2,1)} %constant_dynamic-update-slice_fusion, bf16[3,1024,768]{2,1,0:T(8,128)(2,1)} %get-tuple-element.174), kind=kOutput, calls=%fused_computation.108 | convolution fusion | flops 3624468480 | bytes 10616832 | tf_op jit(solution)/shard_map/bsd,bsf->df/dot_general | solution.py:139
  282.1 7.3 %bitcast_convert_fusion = bf16[768,768]{1,0:T(8,128)(2,1)} fusion(bf16[3,1024,768]{2,1,0:T(8,128)(2,1)S(1)} %bitcast.227, bf16[3,1024,768]{2,1,0:T(8,128)(2,1)} %all-gather.2.cloned.1.call-done), kind=kOutput, calls=%fused_computation.107 | convolution fusion | flops 3624468480 | bytes 10616832 | tf_op jit(solution)/shard_map/bsf,bsd->fd/dot_general | solution.py:134
  289.6 5.9 %fusion.81 = f32[3,1024,768]{2,1,0:T(8,128)S(1)} fusion(bf16[3,1024,768]{2,1,0:T(8,128)(2,1)} %get-tuple-element.174, bf16[768,768]{1,0:T(8,128)(2,1)S(1)} %copy-done), kind=kOutput, calls=%fused_computation.136 | convolution fusion | flops 3623878656 | bytes 15335424 | tf_op jit(solution)/shard_map/bsf,df->bsd/dot_general | solution.py:141
  295.5 5.6 add_convert_fusion
  301.3 6.1 %fusion.79 = f32[3,1024,768]{2,1,0:T(8,128)S(1)} fusion(bf16[3,1024,768]{2,1,0:T(8,128)(2,1)} %get-tuple-element.159, bf16[768,768]{1,0:T(8,128)(2,1)S(1)} %copy-done.46), kind=kOutput, calls=%fused_computation.134 | convolution fusion | flops 3623878656 | bytes 15335424 | tf_op jit(solution)/shard_map/bsf,fd->bsd/dot_general | solution.py:126
  312.3 28.2 %all-reduce.1 = (bf16[3,64]{1,0:T(4,128)(2,1)S(1)}, bf16[3,64]{1,0:T(4,128)(2,1)S(1)}, bf16[768]{0:T(1024)(128)(2,1)S(1)}) all-reduce(bf16[3,64]{1,0:T(4,128)(2,1)S(1)} %get-tuple-element.176, bf16[3,64]{1,0:T(4,128)(2,1)S(1)} %get-tuple-element.110, bf16[768]{0:T(1024)(128)(2,1)S(1)} %get-tuple-element.173), channel_id=1, replica_groups=mesh['tp'=4,'dp'=8] {'dp'}, use_global_device_ids=true, to_apply=%region_25.26 | all-reduce | flops 1152 | bytes 4608 | tf_op jit(solution)/shard_map/psum | solution.py:176
  342.3 98.0 %all-reduce.5.cloned.1.call-done = (bf16[768,576]{0,1:T(8,128)(2,1)}, bf16[192,768]{1,0:T(8,128)(2,1)}, bf16[768,768]{1,0:T(8,128)(2,1)}, bf16[768,768]{1,0:T(8,128)(2,1)}) async-done(((bf16[768,576]{0,1:T(8,128)(2,1)}, bf16[192,768]{1,0:T(8,128)(2,1)}, bf16[768,768]{1,0:T(8,128)(2,1)}, bf16[768,768]{1,0:T(8,128)(2,1)}), (bf16[768,576]{0,1:T(8,128)(2,1)}, bf16[192,768]{1,0:T(8,128)(2,1)}, ...) | async-done | bytes 3538960 | tf_op jit(solution)/shard_map/psum | solution.py:175
  447.0 42.7 %reduce-scatter.5.cloned.1.call-done = bf16[3,256,768]{2,1,0:T(8,128)(2,1)} async-done(((bf16[3,1024,768]{2,1,0:T(8,128)(2,1)}), bf16[3,256,768]{2,1,0:T(8,128)(2,1)}) %reduce-scatter.5.cloned.1.call-update) | async-done | bytes 1179664 | tf_op jit(solution)/shard_map/reduce_scatter | solution.py:166
  495.0 45.0 %reduce-scatter.3.cloned.1.call-done = bf16[3,256,768]{2,1,0:T(8,128)(2,1)} async-done(((bf16[3,1024,768]{2,1,0:T(8,128)(2,1)}), bf16[3,256,768]{2,1,0:T(8,128)(2,1)}) %reduce-scatter.3.cloned.1.call-update) | async-done | bytes 1179664 | tf_op jit(solution)/shard_map/reduce_scatter | solution.py:129
  544.5 39.6 %all-reduce = (f32[768]{0:T(1024)}, f32[768]{0:T(1024)}) all-reduce(f32[768]{0:T(1024)} %get-tuple-element.114, f32[768]{0:T(1024)} %get-tuple-element.169), channel_id=1, replica_groups=mesh['tp'=4,'dp'=8] {'tp','dp'}, use_global_device_ids=true, to_apply=%region_22.23 | all-reduce | flops 1536 | bytes 12288 | tf_op jit(solution)/shard_map/psum | solution.py:173
  (226 shorter events, 169.8 us)
Async XLA Ops:
  7.2 99.4 %copy-start = (bf16[768,768]{1,0:T(8,128)(2,1)S(1)}, bf16[768,768]{1,0:T(8,128)(2,1)}, u32[]{:S(2)}) copy-start(bf16[768,768]{1,0:T(8,128)(2,1)} %param.23) | copy-start | bytes 3538948
  7.2 135.4 %all-gather.2.cloned.1.call-start = ((), (), s32[]{:S(2)}) async-start(), calls=%async_computation.3 | async-start | bytes 5898240 | tf_op jit(solution)/shard_map/all_gather | solution.py:133
  8.9 29.3 %copy-start.33 = (f32[3,256]{1,0:T(4,128)}, f32[3,256]{1,0:T(4,128)S(1)}, u32[]{:S(2)}) copy-start(f32[3,256]{1,0:T(4,128)S(1)} %broadcast_multiply_fusion.2) | copy-start | bytes 9220
  11.3 27.0 %copy-start.37 = (f32[3,256]{1,0:T(4,128)}, f32[3,256]{1,0:T(4,128)S(1)}, u32[]{:S(2)}) copy-start(f32[3,256]{1,0:T(4,128)S(1)} %fusion.94) | copy-start | bytes 9220
  11.7 26.5 %collective-permute-start = (bf16[3,256,768]{2,1,0:T(8,128)(2,1)S(1)}, bf16[3,256,768]{2,1,0:T(8,128)(2,1)}, u32[]{:S(2)}, u32[]{:S(2)}) collective-permute-start(bf16[3,256,768]{2,1,0:T(8,128)(2,1)S(1)} %fusion.65), channel_id=1, source_target_pairs={{0,8},{8,16},{16,24},{24,0},{1,9},{9,17},{17,25},{25,1},{2,10},{10... | collective-permute-start | bytes 3538952 | tf_op jit(solution)/shard_map/ppermute | solution.py:23
  12.3 38.2 %collective-permute-start.1 = (bf16[3,256,768]{2,1,0:T(8,128)(2,1)S(1)}, bf16[3,256,768]{2,1,0:T(8,128)(2,1)}, u32[]{:S(2)}, u32[]{:S(2)}) collective-permute-start(bf16[3,256,768]{2,1,0:T(8,128)(2,1)S(1)} %fusion.65), channel_id=1, source_target_pairs={{0,24},{8,0},{16,8},{24,16},{1,25},{9,1},{17,9},{25,17},{2,26},{10... | collective-permute-start | bytes 3538952 | tf_op jit(solution)/shard_map/ppermute | solution.py:30
  38.2 17.8 %collective-permute-start.2 = (bf16[3,256,768]{2,1,0:T(8,128)(2,1)}, bf16[3,256,768]{2,1,0:T(8,128)(2,1)}, u32[]{:S(2)}, u32[]{:S(2)}) collective-permute-start(bf16[3,256,768]{2,1,0:T(8,128)(2,1)} %collective-permute-done), channel_id=1, source_target_pairs={{0,8},{8,16},{16,24},{24,0},{1,9},{9,17},{17,25},{25,1},{2,10},{10... | collective-permute-start | bytes 3538952 | tf_op jit(solution)/shard_map/ppermute | solution.py:23
  40.6 399.7 %all-reduce.5.cloned.1.call-start = ((), (), s32[]{:S(2)}) async-start(), calls=%async_computation.5 | async-start | bytes 7077888 | tf_op jit(solution)/shard_map/psum | solution.py:175
  69.3 37.3 %copy-start.44 = (f32[768]{0:T(1024)S(1)}, f32[768]{0:T(1024)}, u32[]{:S(2)}) copy-start(f32[768]{0:T(1024)} %param.24) | copy-start | bytes 9220
  106.6 9.4 %copy-start.8 = (bf16[3,1024,3,64]{1,3,2,0:T(8,128)(2,1)}, bf16[3,1024,3,64]{1,3,2,0:T(8,128)(2,1)S(1)}, u32[]{:S(2)}) copy-start(bf16[3,1024,3,64]{1,3,2,0:T(8,128)(2,1)S(1)} %get-tuple-element.393) | copy-start | bytes 3538948
  106.6 9.4 %copy-start.9 = (bf16[3,1024,3,64]{1,3,2,0:T(8,128)(2,1)}, bf16[3,1024,3,64]{1,3,2,0:T(8,128)(2,1)S(1)}, u32[]{:S(2)}) copy-start(bf16[3,1024,3,64]{1,3,2,0:T(8,128)(2,1)S(1)} %get-tuple-element.394) | copy-start | bytes 3538948
  119.6 23.0 %copy-start.31 = (bf16[192,768]{1,0:T(8,128)(2,1)S(1)}, bf16[192,768]{1,0:T(8,128)(2,1)}, u32[]{:S(2)}) copy-start(bf16[192,768]{1,0:T(8,128)(2,1)} %param.22) | copy-start | bytes 884740
  147.6 88.0 %copy-start.5 = (f32[3,1024,3,1,64]{1,4,3,2,0:T(8,128)S(1)}, f32[3,1024,3,1,64]{1,4,3,2,0:T(8,128)}, u32[]{:S(2)}) copy-start(f32[3,1024,3,1,64]{1,4,3,2,0:T(8,128)} %copy-done.4) | copy-start | bytes 7077892
  147.6 88.0 %copy-start.41 = (f32[3,64]{1,0:T(4,128)S(1)}, f32[3,64]{1,0:T(4,128)}, u32[]{:S(2)}) copy-start(f32[3,64]{1,0:T(4,128)} %param.20) | copy-start | bytes 2308
  246.1 8.5 %slice-start = ((s8[9437184]{0:T(1024)(128)(4,1)}), s8[4194304]{0:T(1024)(128)(4,1)S(1)}, s32[]{:S(2)}) async-start(s8[9437184]{0:T(1024)(128)(4,1)} %bitcast.222), calls=%async_computation.6 | async-start | bytes 8388608
  246.7 7.9 %copy-start.14 = (bf16[3,1024,3,3,64]{1,4,3,2,0:T(8,128)(2,1)}, bf16[3,1024,3,3,64]{1,4,3,2,0:T(8,128)(2,1)S(1)}, u32[]{:S(2)}) copy-start(bf16[3,1024,3,3,64]{1,4,3,2,0:T(8,128)(2,1)S(1)} %copy.36) | copy-start | bytes 10616836
  246.8 35.4 %slice-start.3 = ((s8[4718592]{0:T(1024)(128)(4,1)}), s8[4194304]{0:T(1024)(128)(4,1)S(1)}, s32[]{:S(2)}) async-start(s8[4718592]{0:T(1024)(128)(4,1)} %bitcast.226), calls=%async_computation.9 | async-start | bytes 8388608
  254.7 27.5 %slice-start.4 = ((s8[4718592]{0:T(1024)(128)(4,1)}), s8[524288]{0:T(1024)(128)(4,1)S(1)}, s32[]{:S(2)}) async-start(s8[4718592]{0:T(1024)(128)(4,1)} %bitcast.226), calls=%async_computation.10 | async-start | bytes 1048576
  289.5 200.3 %reduce-scatter.5.cloned.1.call-start = ((), (), s32[]{:S(2)}) async-start(), calls=%async_computation.4 | async-start | bytes 5898240 | tf_op jit(solution)/shard_map/reduce_scatter | solution.py:166
  301.2 238.8 %reduce-scatter.3.cloned.1.call-start = ((), (), s32[]{:S(2)}) async-start(), calls=%async_computation.2 | async-start | bytes 5898240 | tf_op jit(solution)/shard_map/reduce_scatter | solution.py:129
  444.8 45.0 %copy-start.7 = (bf16[3,256,768]{2,1,0:T(8,128)(2,1)S(1)}, bf16[3,256,768]{2,1,0:T(8,128)(2,1)}, u32[]{:S(2)}) copy-start(bf16[3,256,768]{2,1,0:T(8,128)(2,1)} %param.16) | copy-start | bytes 3538948
  444.8 45.0 %copy-start.34 = (f32[3,256]{1,0:T(4,128)S(1)}, f32[3,256]{1,0:T(4,128)}, u32[]{:S(2)}) copy-start(f32[3,256]{1,0:T(4,128)} %copy-done.33) | copy-start | bytes 9220
  444.8 45.0 %copy-start.36 = (f32[768]{0:T(1024)S(1)}, f32[768]{0:T(1024)}, u32[]{:S(2)}) copy-start(f32[768]{0:T(1024)} %param.18) | copy-start | bytes 9220
  444.8 47.7 %copy-start.38 = (f32[3,256]{1,0:T(4,128)S(1)}, f32[3,256]{1,0:T(4,128)}, u32[]{:S(2)}) copy-start(f32[3,256]{1,0:T(4,128)} %copy-done.37) | copy-start | bytes 9220
  (40 other events, 135.0 us)
Sparse Core Ops, SparseCore 0:
  40.7 41.0 all-gather.1
  289.6 150.6 all-reduce.4
  442.8 46.8 reduce-scatter.4
  492.2 47.8 reduce-scatter.2
